TPU v7x, 128 devices: a whole 4x4x4 slice. The times are simulated.
128 devices in a mesh: req: 64 (over z, x, y), kv: 2 (over core).
Axes of the slice: x: 4, y: 4, z: 4, core: 2. Of those that a mesh axis runs over, the one named last changes fastest.
Arguments:
- tokens: bfloat16 [1024, 1536], P('req'), may hold values from -6 to 6
- gain_attn: bfloat16 [1536], replicated, may hold values from 0.099609375 to 1.8984375
- w_query: bfloat16 [1536, 1536], P(None, 'kv'), may hold values from -0.15625 to 0.15625
- w_key: bfloat16 [1536, 256], P(None, 'kv'), may hold values from -0.15625 to 0.15625
- w_value: bfloat16 [1536, 256], P(None, 'kv'), may hold values from -0.15625 to 0.15625
- w_out: bfloat16 [1536, 1536], P('kv'), may hold values from -0.15625 to 0.15625
- cache_k: bfloat16 [4096, 128, 256], P('req', None, 'kv'), may hold values from -720 to 720
- cache_v: bfloat16 [4096, 128, 256], P('req', None, 'kv'), may hold values from -6 to 6
- page_table: int32 [1024, 4], P('req'), may hold values from 0 to 63, as said below
- lengths: int32 [1024], replicated, may hold values from 1 to 512, as said below
- new_owner: int32 [64], replicated, may hold values from 0 to 63, as said below
- gain_moe: bfloat16 [1536], replicated, may hold values from 0.099609375 to 1.8984375
- w_router: bfloat16 [1536, 32], replicated, may hold values from -0.15625 to 0.15625
- routes: int32 [1024, 4], P(('req', 'kv')), may hold values from 0 to 31, all different within a row; in each aligned block of 8 rows (0 to 7, 8 to 15, ...) at most 2 rows name the same one
- w_gate: bfloat16 [64, 1536, 384], P('req', None, 'kv'), may hold values from -0.15625 to 0.15625
- w_up: bfloat16 [64, 1536, 384], P('req', None, 'kv'), may hold values from -0.15625 to 0.15625
- w_down: bfloat16 [64, 1536, 384], P('req', None, 'kv'), may hold values from -0.21875 to 0.21875
Outputs:
- layer_out: bfloat16 [1024, 1536], P(('req', 'kv'))
Inputs may be any that keep to these rules, and one draw needn't show every extreme that they name: `lengths`: the last slot of each device (15, 31, ...) holds at most 256, and some last slot holds exactly 256; some length equals 512. `page_table`: the page indices of the 16 slots of one device are together a permutation of 0 to 63. `new_owner`: A permutation of the devices of req. `routes`: in each aligned block of 8 rows (the rows of one device) no expert is named by more than 2 rows.
All inputs are finite; a program needn't handle non-finite values.
Results may differ from a plain program's by a relative error of at most 0.015.
The roundings to bfloat16 on the way count: a program that leaves them out, or rounds other values in their place, can miss the bound.
Values may be sent and summed in bfloat16 or wider, within the bound.
A program may use at most 128 MiB of HBM per device.

v0:
```python
import jax
import jax.numpy as jnp
from jax import lax
from jax.sharding import PartitionSpec as P

MOVE_LEN = 256


def rms_scaled(values, gain_vec):
    wide = values.astype(jnp.float32)
    squares = jnp.mean(wide * wide, axis=-1, keepdims=True)
    return (wide * lax.rsqrt(squares + 1e-06) * gain_vec.astype(jnp.float32)).astype(jnp.bfloat16)


def cache_partial(queries, page_keys, page_values, live_len):
    inv_root = queries.shape[-1] ** (-0.5)
    scores = (
        jnp.einsum("rgd,rtd->rgt", queries, page_keys, preferred_element_type=jnp.float32)
        * inv_root
    )
    positions = lax.broadcasted_iota(jnp.int32, scores.shape, 2)
    live_mask = positions < live_len[:, None, None]
    scores = jnp.where(live_mask, scores, -1e30)
    top_score = jnp.max(scores, axis=-1)
    weights = jnp.where(live_mask, jnp.exp(scores - top_score[..., None]), 0.0)
    totals = jnp.sum(weights, axis=-1)
    accumulated = jnp.einsum(
        "rgt,rtd->rgd",
        weights.astype(jnp.bfloat16),
        page_values,
        preferred_element_type=jnp.float32,
    )
    return (accumulated, top_score, totals)


def finish_heads(accumulated, top_score, totals, queries, key_now, value_now):
    inv_root = queries.shape[-1] ** (-0.5)
    own_score = (
        jnp.einsum("rgd,rd->rg", queries, key_now, preferred_element_type=jnp.float32) * inv_root
    )
    joint_max = jnp.maximum(top_score, own_score)
    old_part = jnp.exp(top_score - joint_max)
    new_part = jnp.exp(own_score - joint_max)
    merged = (
        accumulated * old_part[..., None]
        + new_part[..., None] * value_now.astype(jnp.float32)[:, None, :]
    )
    result = merged / (totals * old_part + new_part)[..., None]
    return result.astype(jnp.bfloat16).reshape(queries.shape[0], -1)


def shards(
    tokens,
    gain_attn,
    w_query,
    w_key,
    w_value,
    w_out,
    cache_k,
    cache_v,
    page_table,
    lengths,
    new_owner,
    gain_moe,
    w_router,
    routes,
    w_gate,
    w_up,
    w_down,
):
    req_dev = tokens.shape[0]
    half_rows = req_dev // 2
    req_count = lax.axis_size("req")
    req_index = lax.axis_index("req")
    kv_index = lax.axis_index("kv")
    last_slot = req_dev - 1
    normed = rms_scaled(tokens, gain_attn)
    head_dim = w_key.shape[1]
    groups = w_query.shape[1] // head_dim
    queries = (
        jnp.dot(normed, w_query, preferred_element_type=jnp.float32)
        .astype(jnp.bfloat16)
        .reshape(req_dev, groups, head_dim)
    )
    key_now = jnp.dot(normed, w_key, preferred_element_type=jnp.float32).astype(jnp.bfloat16)
    value_now = jnp.dot(normed, w_value, preferred_element_type=jnp.float32).astype(jnp.bfloat16)
    own_len = lax.dynamic_slice_in_dim(lengths, req_index * req_dev, req_dev)
    page_keys = cache_k[page_table].reshape(req_dev, -1, head_dim)
    page_values = cache_v[page_table].reshape(req_dev, -1, head_dim)
    peer_ids = jnp.arange(req_count, dtype=jnp.int32)
    target = new_owner[req_index]
    source = jnp.sum(jnp.where(new_owner == req_index, peer_ids, 0))
    empty_bf = jnp.zeros((), jnp.bfloat16)
    chosen = (peer_ids == target)[:, None, None]
    outgoing_k = jnp.where(chosen, page_keys[last_slot, :MOVE_LEN][None], empty_bf)
    outgoing_v = jnp.where(chosen, page_values[last_slot, :MOVE_LEN][None], empty_bf)
    arrived_k, arrived_v = (
        lax.all_to_all(outgoing_k, "req", split_axis=0, concat_axis=0, tiled=True),
        lax.all_to_all(outgoing_v, "req", split_axis=0, concat_axis=0, tiled=True),
    )
    page_keys = page_keys.at[last_slot, :MOVE_LEN].set(arrived_k[source])
    page_values = page_values.at[last_slot, :MOVE_LEN].set(arrived_v[source])
    live_len = own_len.at[last_slot].set(lengths[source * req_dev + last_slot])
    accumulated, top_score, totals = cache_partial(queries, page_keys, page_values, live_len)
    attended = finish_heads(accumulated, top_score, totals, queries, key_now, value_now)
    head_terms = jnp.dot(attended, w_out, preferred_element_type=jnp.float32)
    head_total = lax.psum_scatter(head_terms, "kv", scatter_dimension=0, tiled=True)
    residual = lax.dynamic_slice_in_dim(tokens, kv_index * half_rows, half_rows, 0)
    middle = (residual.astype(jnp.float32) + head_total).astype(jnp.bfloat16)
    normed_two = rms_scaled(middle, gain_moe)
    logits = jnp.dot(normed_two, w_router, preferred_element_type=jnp.float32)
    route_weight = jax.nn.softmax(jnp.take_along_axis(logits, routes, axis=1), axis=-1)
    experts = req_count // 2
    topk = routes.shape[1]
    capacity = max(2, half_rows * topk // experts)
    flat_routes = routes.reshape(-1)
    onehot = (flat_routes[:, None] == jnp.arange(experts, dtype=jnp.int32)[None, :]).astype(
        jnp.int32
    )
    slot_rank = jnp.sum((jnp.cumsum(onehot, axis=0) - onehot) * onehot, axis=1)
    expert_of_peer = peer_ids // 2
    slot_ids = jnp.arange(capacity, dtype=jnp.int32)
    placement_map = (flat_routes[None, None, :] == expert_of_peer[:, None, None]) & (
        slot_rank[None, None, :] == slot_ids[None, :, None]
    )
    placement_map = placement_map.astype(jnp.float32).reshape(req_count, capacity, half_rows, topk)
    picked = jnp.sum(placement_map, axis=-1)
    blending = jnp.sum(placement_map * route_weight[None, None], axis=-1)
    outgoing = jnp.einsum(
        "pci,id->pcd", picked.astype(jnp.bfloat16), normed_two, preferred_element_type=jnp.float32
    ).astype(jnp.bfloat16)
    gate_half, up_half, down_half = (
        lax.all_gather(w_gate, "kv", axis=2, tiled=True),
        lax.all_gather(w_up, "kv", axis=2, tiled=True),
        lax.all_gather(w_down, "kv", axis=2, tiled=True),
    )
    received = lax.all_to_all(outgoing, "req", split_axis=0, concat_axis=0, tiled=True)
    senders, slot_count, feature_count = received.shape
    flat_rows = received.reshape(senders * slot_count, feature_count)
    gate_val = jnp.dot(flat_rows, gate_half[0], preferred_element_type=jnp.float32)
    up_val = jnp.dot(flat_rows, up_half[0], preferred_element_type=jnp.float32)
    hidden = (jax.nn.relu(gate_val) * up_val).astype(jnp.bfloat16)
    result = lax.dot_general(
        hidden, down_half[0], (((1,), (1,)), ((), ())), preferred_element_type=jnp.float32
    )
    returned = lax.all_to_all(
        result.reshape(senders, slot_count, feature_count),
        "req",
        split_axis=0,
        concat_axis=0,
        tiled=True,
    )
    mixed = jnp.einsum("pci,pcd->id", blending, returned, precision=lax.Precision.HIGHEST)
    return (middle.astype(jnp.float32) + mixed).astype(jnp.bfloat16)


def solution(mesh):
    return jax.shard_map(
        shards,
        mesh=mesh,
        in_specs=(
            P("req", None),
            P(),
            P(None, "kv"),
            P(None, "kv"),
            P(None, "kv"),
            P("kv", None),
            P("req", None, "kv"),
            P("req", None, "kv"),
            P("req", None),
            P(),
            P(),
            P(),
            P(),
            P(("req", "kv"), None),
            P("req", None, "kv"),
            P("req", None, "kv"),
            P("req", None, "kv"),
        ),
        out_specs=P(("req", "kv"), None),
        check_vma=False,
    )
```

profile of v0, /device:TPU:0, one launch (start us, length us, event | category | flops | bytes accessed | tf_op | source)
XLA Modules:
  0.0 236.1 jit_solution(13709867377025384650)
XLA Ops:
  6.5 1.4 dynamic_slice.21
  9.5 3.7 %gather_fusion = bf16[64,128,128]{2,1,0:T(8,128)(2,1)} fusion(bf16[64,128,128]{2,1,0:T(8,128)(2,1)} %param.29, s32[1024]{0:T(1024)S(1)} %pad_clamp_fusion), kind=kCustom, calls=%fused_computation | custom fusion | bytes 4194560 | tf_op jit(solution)/shard_map/gather | solution.py:88
  13.2 3.8 %gather_fusion.1 = bf16[64,128,128]{2,1,0:T(8,128)(2,1)} fusion(bf16[64,128,128]{2,1,0:T(8,128)(2,1)} %param.30, s32[1024]{0:T(1024)S(1)} %pad_clamp_fusion), kind=kCustom, calls=%fused_computation.1 | custom fusion | bytes 4194560 | tf_op jit(solution)/shard_map/gather | solution.py:89
  17.0 0.9 slice_bitcast_fusion
  17.8 2.6 %broadcast_select_fusion.1 = (bf16[64,256,128]{2,1,0:T(8,128)(2,1)S(1)}, bf16[64,256,128]{2,1,0:T(8,128)(2,1)}) fusion(pred[64]{0:T(512)(128)(4,1)S(1)} %iota_compare_fusion.3, bf16[256,128]{1,0:T(8,128)(2,1)S(1)} %get-tuple-element.53, bf16[256,128]{1,0:T(8,128)(2,1)S(1)} %get-tuple-element.52), kind=kLoop, calls=%fused_computation.4 | loop fusion | flops 4194304 | bytes 8519744 | tf_op jit(solution)/shard_map/jit(_where)/select_n | solution.py:95
  20.4 63.5 %all_to_all.20 = bf16[64,256,128]{2,1,0:T(8,128)(2,1)} all-to-all(bf16[64,256,128]{2,1,0:T(8,128)(2,1)S(1)} %get-tuple-element.48), channel_id=1, replica_groups=mesh['req'=64,'kv'=2] {'req'}, dimensions={0} | all-to-all | bytes 8388608 | tf_op jit(solution)/shard_map/all_to_all | solution.py:98
  83.9 6.6 %all-to-all-start.1 = ((bf16[64,256,128]{2,1,0:T(8,128)(2,1)}), bf16[64,256,128]{2,1,0:T(8,128)(2,1)}, u32[]{:S(2)}, u32[]{:S(2)}) async-start(bf16[64,256,128]{2,1,0:T(8,128)(2,1)} %get-tuple-element.49), calls=%async_computation.1 | async-start | bytes 8388608 | tf_op jit(solution)/shard_map/all_to_all | solution.py:99
  93.3 2.1 convolution_convert_fusion.1
  98.4 1.5 dynamic-slice_dynamic-update-slice_fusion.1
  99.8 2.3 fusion.62
  102.4 38.8 %all-to-all-done.1 = bf16[64,256,128]{2,1,0:T(8,128)(2,1)} async-done(((bf16[64,256,128]{2,1,0:T(8,128)(2,1)}), bf16[64,256,128]{2,1,0:T(8,128)(2,1)}, u32[]{:S(2)}, u32[]{:S(2)}) %all-to-all-start.1) | async-done | bytes 4194336 | tf_op jit(solution)/shard_map/all_to_all | solution.py:99
  141.2 1.5 dynamic-slice_dynamic-update-slice_fusion
  142.7 2.0 fusion.20
  144.7 1.1 fusion.39
  148.9 5.7 %reduce-scatter.2.cloned.1.call-done = f32[8,1536]{1,0:T(8,128)} async-done(((f32[16,1536]{1,0:T(8,128)}), f32[8,1536]{1,0:T(8,128)}) %reduce-scatter.2.cloned.1.call-update) | async-done | bytes 49168 | tf_op jit(solution)/shard_map/reduce_scatter | solution.py:107
  154.6 0.9 fusion.34
  157.8 22.7 %all_to_all.21 = bf16[64,2,1536]{2,1,0:T(2,128)(2,1)S(1)} all-to-all(bf16[64,2,1536]{2,1,0:T(2,128)(2,1)S(1)} %copy.70), channel_id=1, replica_groups=mesh['req'=64,'kv'=2] {'req'}, dimensions={0} | all-to-all | bytes 786432 | tf_op jit(solution)/shard_map/all_to_all | solution.py:137
  180.7 1.8 fusion.4
  182.6 2.1 all-gather.4.cloned.1.call-done
  184.6 1.8 fusion.15
  186.5 13.0 %all-gather.8.cloned.1.call-done = bf16[1,1536,384]{1,2,0:T(8,128)(2,1)} async-done(((bf16[1,1536,192]{1,2,0:T(8,128)(2,1)}), bf16[1,1536,384]{1,2,0:T(8,128)(2,1)}) %all-gather.8.cloned.1.call-update) | async-done | bytes 1179664 | tf_op jit(solution)/shard_map/all_gather | solution.py:135
  199.4 1.6 fusion.2
  201.7 26.7 %all_to_all.22 = f32[64,2,1536]{2,1,0:T(2,128)S(1)} all-to-all(f32[64,2,1536]{2,1,0:T(2,128)S(1)} %copy.73), channel_id=1, replica_groups=mesh['req'=64,'kv'=2] {'req'}, dimensions={0} | all-to-all | bytes 1572864 | tf_op jit(solution)/shard_map/all_to_all | solution.py:146
  228.4 1.2 fusion.1
  (74 shorter events, 10.9 us)
Async XLA Ops:
  6.5 138.2 %copy-start = (bf16[768,1536]{1,0:T(8,128)(2,1)S(1)}, bf16[768,1536]{1,0:T(8,128)(2,1)}, u32[]{:S(2)}) copy-start(bf16[768,1536]{1,0:T(8,128)(2,1)} %param.28) | copy-start | bytes 7077892
  83.9 6.7 %copy-start.8 = (s32[64]{0:T(128)S(1)}, s32[64]{0:T(128)}, u32[]{:S(2)}) copy-start(s32[64]{0:T(128)} %param.33) | copy-start | bytes 772
  83.9 9.2 %copy-start.5 = (bf16[1536]{0:T(1024)(128)(2,1)S(1)}, bf16[1536]{0:T(1024)(128)(2,1)}, u32[]{:S(2)}) copy-start(bf16[1536]{0:T(1024)(128)(2,1)} %param.24) | copy-start | bytes 9220
  83.9 9.3 %copy-start.1 = (bf16[16,1536]{1,0:T(8,128)(2,1)S(1)}, bf16[16,1536]{1,0:T(8,128)(2,1)}, u32[]{:S(2)}) copy-start(bf16[16,1536]{1,0:T(8,128)(2,1)} %param.23) | copy-start | bytes 147460
  83.9 57.3 %all-to-all-start.1 = ((bf16[64,256,128]{2,1,0:T(8,128)(2,1)}), bf16[64,256,128]{2,1,0:T(8,128)(2,1)}, u32[]{:S(2)}, u32[]{:S(2)}) async-start(bf16[64,256,128]{2,1,0:T(8,128)(2,1)} %get-tuple-element.49), calls=%async_computation.1 | async-start | bytes 8388608 | tf_op jit(solution)/shard_map/all_to_all | solution.py:99
  90.5 7.3 %copy-start.2 = (bf16[1536,128]{1,0:T(8,128)(2,1)S(1)}, bf16[1536,128]{1,0:T(8,128)(2,1)}, u32[]{:S(2)}) copy-start(bf16[1536,128]{1,0:T(8,128)(2,1)} %param.26) | copy-start | bytes 1179652
  90.5 7.6 %copy-start.3 = (bf16[1536,128]{1,0:T(8,128)(2,1)S(1)}, bf16[1536,128]{1,0:T(8,128)(2,1)}, u32[]{:S(2)}) copy-start(bf16[1536,128]{1,0:T(8,128)(2,1)} %param.27) | copy-start | bytes 1179652
  90.5 64.1 %reduce-scatter.2.cloned.1.call-start = ((), (), s32[]{:S(2)}) async-start(), calls=%async_computation.5 | async-start | bytes 147456 | tf_op jit(solution)/shard_map/reduce_scatter | solution.py:107
  144.7 3.2 %copy-start.4 = (s32[8,4]{0,1:T(4,128)S(1)}, s32[8,4]{0,1:T(4,128)}, u32[]{:S(2)}) copy-start(s32[8,4]{0,1:T(4,128)} %param.36) | copy-start | bytes 388
  144.7 3.4 %copy-start.6 = (bf16[1536]{0:T(1024)(128)(2,1)S(1)}, bf16[1536]{0:T(1024)(128)(2,1)}, u32[]{:S(2)}) copy-start(bf16[1536]{0:T(1024)(128)(2,1)} %param.34) | copy-start | bytes 9220
  144.7 10.8 %copy-start.7 = (bf16[1536,32]{0,1:T(8,128)(2,1)S(1)}, bf16[1536,32]{0,1:T(8,128)(2,1)}, u32[]{:S(2)}) copy-start(bf16[1536,32]{0,1:T(8,128)(2,1)} %param.35) | copy-start | bytes 294916
  145.8 34.9 %all-gather.6.cloned.1.call-start = ((), (), s32[]{:S(2)}) async-start(), calls=%async_computation.7 | async-start | bytes 1769472 | tf_op jit(solution)/shard_map/all_gather | solution.py:134
  146.6 38.1 %all-gather.4.cloned.1.call-start = ((), (), s32[]{:S(2)}) async-start(), calls=%async_computation.6 | async-start | bytes 1769472 | tf_op jit(solution)/shard_map/all_gather | solution.py:133
  147.3 52.1 %all-gather.8.cloned.1.call-start = ((), (), s32[]{:S(2)}) async-start(), calls=%async_computation.8 | async-start | bytes 1769472 | tf_op jit(solution)/shard_map/all_gather | solution.py:135
Sparse Core Ops, SparseCore 0:
  145.9 8.5 reduce-scatter.1
  156.2 13.4 all-gather.5
  171.3 13.2 all-gather.3
  186.1 13.2 all-gather.7
where the time goes:
time: 237 us; the launch traced here: 236 us
  blocking collectives  113 us (48%)
  waiting for transfers between devices  61.4 us (26%)
  local copies, waits for them, and re-layouts  17.2 us (7%)
  between operations  16 us (7%)
  matrix products  15.1 us (6%)
  other arithmetic  6.77 us (3%)
  starting transfers between devices  6.72 us (3%)
    all_to_all x1, blocking collectives, shards(): lax.all_to_all(outgoing_k, 'req', split_axis=0, concat_axis=0, tiled=True)  63.5 us
    all_to_all x1, waiting for transfers between devices, shards(): lax.all_to_all(outgoing_v, 'req', split_axis=0, concat_axis=0, tiled=True)  38.8 us
    all_to_all x1, blocking collectives, shards(): lax.all_to_all(result.reshape(senders, slot_count, feature_count), 'req',...  26.7 us
    all_to_all x1, blocking collectives, shards(): lax.all_to_all(outgoing, 'req', split_axis=0, concat_axis=0, tiled=True)  22.7 us
    all_gather x1, waiting for transfers between devices, shards(): lax.all_gather(w_down, 'kv', axis=2, tiled=True)  13 us
    all_to_all x1, starting transfers between devices, shards(): lax.all_to_all(outgoing_v, 'req', split_axis=0, concat_axis=0, tiled=True)  6.56 us
    reduce_scatter x1, waiting for transfers between devices, shards(): lax.psum_scatter(head_terms, 'kv', scatter_dimension=0, tiled=True)  5.66 us
  transfers between devices with their start and end apart: 5, of which 4 were waited for; matrix products, arithmetic and copies ran while one was open for 7% of the time, Pallas kernels for 0%

commit v1 on v0

--- a/solution.py
+++ b/solution.py
@@ -132,7 +132,9 @@
     gate_half, up_half, down_half = (
         lax.all_gather(w_gate, "kv", axis=2, tiled=True),
         lax.all_gather(w_up, "kv", axis=2, tiled=True),
-        lax.all_gather(w_down, "kv", axis=2, tiled=True),
+        jnp.concatenate(
+            lax.all_to_all(jnp.stack(lax.axis_size("kv") * [w_down]), "kv", 0, 0), axis=2
+        ),
     )
     received = lax.all_to_all(outgoing, "req", split_axis=0, concat_axis=0, tiled=True)
     senders, slot_count, feature_count = received.shape

time: 237 us -> 227 us (0.958)
  blocking collectives: 113 us -> 84.9 us
  starting transfers between devices: 6.72 us -> 20.8 us
  local copies, waits for them, and re-layouts: 17.2 us -> 22 us
  waiting for transfers between devices: 61.4 us -> 57.7 us
    all_to_all x1 -> x0, blocking collectives: 22.7 us -> none  [shards(): lax.all_to_all(outgoing, 'req', split_axis=0, concat_axis=0, tiled=True)]
    all_to_all x0 -> x2, starting transfers between devices: none -> 14.1 us  [the longest x1 10.5 us: shards(): lax.all_to_all(outgoing, 'req', split_axis=0, concat_axis=0, tiled=True)]
    all_gather x1 -> x0, waiting for transfers between devices: 13 us -> none  [shards(): lax.all_gather(w_down, 'kv', axis=2, tiled=True)]
    all_to_all x0 -> x2, waiting for transfers between devices: none -> 11.3 us  [the longest x1 11.3 us: shards(): lax.all_to_all(outgoing, 'req', split_axis=0, concat_axis=0, tiled=True)]
    all_to_all x1, blocking collectives: 26.7 us -> 21.5 us  [shards(): lax.all_to_all(result.reshape(senders, slot_count, feature_count), 'req',...]
  transfers between devices with their start and end apart: 5 -> 6, of which waited for: 4 -> 3; matrix products, arithmetic and copies ran while one was open for 7% -> 11% of each run, Pallas kernels for 0% -> 0%
where the time goes in v1:
time: 227 us; the launch traced here: 225 us
  blocking collectives  84.9 us (37%)
  waiting for transfers between devices  57.7 us (25%)
  local copies, waits for them, and re-layouts  22 us (10%)
  starting transfers between devices  20.8 us (9%)
  matrix products  16.2 us (7%)
  between operations  16 us (7%)
  other arithmetic  7.88 us (3%)
    all_to_all x1, blocking collectives, shards(): lax.all_to_all(outgoing_k, 'req', split_axis=0, concat_axis=0, tiled=True)  63.5 us
    all_to_all x1, waiting for transfers between devices, shards(): lax.all_to_all(outgoing_v, 'req', split_axis=0, concat_axis=0, tiled=True)  38.8 us
    all_to_all x1, blocking collectives, shards(): lax.all_to_all(result.reshape(senders, slot_count, feature_count), 'req',...  21.5 us
    all_to_all x1, waiting for transfers between devices, shards(): lax.all_to_all(outgoing, 'req', split_axis=0, concat_axis=0, tiled=True)  11.3 us
    all_to_all x1, starting transfers between devices, shards(): lax.all_to_all(outgoing, 'req', split_axis=0, concat_axis=0, tiled=True)  10.5 us
    all_to_all x1, starting transfers between devices, shards(): lax.all_to_all(outgoing_v, 'req', split_axis=0, concat_axis=0, tiled=True)  6.56 us
    reduce_scatter x1, waiting for transfers between devices, shards(): lax.psum_scatter(head_terms, 'kv', scatter_dimension=0, tiled=True)  6.24 us
  transfers between devices with their start and end apart: 6, of which 3 were waited for; matrix products, arithmetic and copies ran while one was open for 11% of the time, Pallas kernels for 0%

profile of v1, /device:TPU:0, one launch (start us, length us, event | category | flops | bytes accessed | tf_op | source)
XLA Modules:
  0.0 225.5 jit_solution(10843557951506655670)
XLA Ops:
  6.5 1.4 dynamic_slice.21
  9.5 3.7 %gather_fusion = bf16[64,128,128]{2,1,0:T(8,128)(2,1)} fusion(bf16[64,128,128]{2,1,0:T(8,128)(2,1)} %param.29, s32[1024]{0:T(1024)S(1)} %pad_clamp_fusion), kind=kCustom, calls=%fused_computation | custom fusion | bytes 4194560 | tf_op jit(solution)/shard_map/gather | solution.py:88
  13.2 3.8 %gather_fusion.1 = bf16[64,128,128]{2,1,0:T(8,128)(2,1)} fusion(bf16[64,128,128]{2,1,0:T(8,128)(2,1)} %param.30, s32[1024]{0:T(1024)S(1)} %pad_clamp_fusion), kind=kCustom, calls=%fused_computation.1 | custom fusion | bytes 4194560 | tf_op jit(solution)/shard_map/gather | solution.py:89
  17.8 2.6 %broadcast_select_fusion.1 = (bf16[64,256,128]{2,1,0:T(8,128)(2,1)S(1)}, bf16[64,256,128]{2,1,0:T(8,128)(2,1)}) fusion(pred[64]{0:T(512)(128)(4,1)S(1)} %iota_compare_fusion.3, bf16[256,128]{1,0:T(8,128)(2,1)S(1)} %get-tuple-element.53, bf16[256,128]{1,0:T(8,128)(2,1)S(1)} %get-tuple-element.52), kind=kLoop, calls=%fused_computation.4 | loop fusion | flops 4194304 | bytes 8519744 | tf_op jit(solution)/shard_map/jit(_where)/select_n | solution.py:95
  20.4 63.5 %all_to_all.25 = bf16[64,256,128]{2,1,0:T(8,128)(2,1)} all-to-all(bf16[64,256,128]{2,1,0:T(8,128)(2,1)S(1)} %get-tuple-element.48), channel_id=1, replica_groups=mesh['req'=64,'kv'=2] {'req'}, dimensions={0} | all-to-all | bytes 8388608 | tf_op jit(solution)/shard_map/all_to_all | solution.py:98
  83.9 6.6 %all-to-all-start.1 = ((bf16[64,256,128]{2,1,0:T(8,128)(2,1)}), bf16[64,256,128]{2,1,0:T(8,128)(2,1)}, u32[]{:S(2)}, u32[]{:S(2)}) async-start(bf16[64,256,128]{2,1,0:T(8,128)(2,1)} %get-tuple-element.49), calls=%async_computation.1 | async-start | bytes 8388608 | tf_op jit(solution)/shard_map/all_to_all | solution.py:99
  93.3 2.1 convolution_convert_fusion.1
  98.4 1.5 dynamic-slice_dynamic-update-slice_fusion.1
  99.8 2.3 %fusion.61 = (f32[16,6]{1,0:T(8,128)S(1)}, f32[16,6,512]{2,1,0:T(8,128)S(1)}) fusion(bf16[16,6,128]{2,1,0:T(8,128)(2,1)S(1)} %reshape.249, bf16[16,512,128]{2,1,0:T(8,128)(2,1)} %dynamic-slice_dynamic-update-slice_fusion.1, s32[16]{0:T(128)S(1)} %constant_dynamic-update-slice_fusion), kind=kOutput, calls=%fused_computation.96 | convolution fusion | flops 12779424 | bytes 2318784 | tf_op jit(solution)/shard_map/rgd,rtd->rgt/dot_general | solution.py:18
  102.4 38.8 %all-to-all-done.1 = bf16[64,256,128]{2,1,0:T(8,128)(2,1)} async-done(((bf16[64,256,128]{2,1,0:T(8,128)(2,1)}), bf16[64,256,128]{2,1,0:T(8,128)(2,1)}, u32[]{:S(2)}, u32[]{:S(2)}) %all-to-all-start.1) | async-done | bytes 4194336 | tf_op jit(solution)/shard_map/all_to_all | solution.py:99
  141.2 1.5 dynamic-slice_dynamic-update-slice_fusion
  142.7 2.0 fusion.18
  148.3 6.2 %reduce-scatter.2.cloned.1.call-done = f32[8,1536]{1,0:T(8,128)} async-done(((f32[16,1536]{1,0:T(8,128)}), f32[8,1536]{1,0:T(8,128)}) %reduce-scatter.2.cloned.1.call-update) | async-done | bytes 49168 | tf_op jit(solution)/shard_map/reduce_scatter | solution.py:107
  157.4 1.1 copy.84
  158.5 10.5 %all-to-all-start.2 = ((bf16[64,2,1536]{2,1,0:T(2,128)(2,1)}), bf16[64,2,1536]{2,1,0:T(2,128)(2,1)S(1)}, u32[]{:S(2)}, u32[]{:S(2)}) async-start(bf16[64,2,1536]{2,1,0:T(2,128)(2,1)} %copy.84), calls=%async_computation.3 | async-start | bytes 786432 | tf_op jit(solution)/shard_map/all_to_all | solution.py:139
  170.2 11.3 %all-to-all-done.2 = bf16[64,2,1536]{2,1,0:T(2,128)(2,1)S(1)} async-done(((bf16[64,2,1536]{2,1,0:T(2,128)(2,1)}), bf16[64,2,1536]{2,1,0:T(2,128)(2,1)S(1)}, u32[]{:S(2)}, u32[]{:S(2)}) %all-to-all-start.2) | async-done | bytes 393248 | tf_op jit(solution)/shard_map/all_to_all | solution.py:139
  182.2 3.6 %all-to-all-start.3 = ((bf16[2,1,1536,192]{2,3,1,0:T(8,128)(2,1)}), bf16[2,1,1536,192]{2,3,1,0:T(8,128)(2,1)S(1)}, u32[]{:S(2)}, u32[]{:S(2)}) async-start(bf16[2,1,1536,192]{2,3,1,0:T(8,128)(2,1)} %pad_maximum_fusion), calls=%async_computation.4 | async-start | bytes 2359296 | tf_op jit(solution)/shard_map/all_to_all | solution.py:136
  185.8 1.9 reshape.254
  187.7 2.6 %fusion.2 = f32[128,384]{1,0:T(8,128)} fusion(bf16[128,1536]{1,0:T(8,128)(2,1)} %reshape.254, bf16[1,1536,384]{1,2,0:T(8,128)(2,1)} %all-gather.5.cloned.1.call-done), kind=kOutput, calls=%fused_computation.10 | convolution fusion | flops 150994944 | bytes 1769472 | tf_op jit(solution)/shard_map/dot_general | solution.py:143
  190.3 2.5 %fusion.13 = bf16[128,384]{1,0:T(8,128)(2,1)} fusion(f32[128,384]{1,0:T(8,128)} %fusion.2, bf16[128,1536]{1,0:T(8,128)(2,1)} %reshape.254, bf16[1,1536,384]{1,2,0:T(8,128)(2,1)} %all-gather.3.cloned.1.call-done), kind=kOutput, calls=%fused_computation.18 | convolution fusion | flops 151142400 | bytes 1867776 | tf_op jit(solution)/shard_map/dot_general | solution.py:142
  192.8 1.6 dot_general.52
  194.4 1.3 fusion.31
  196.3 21.5 %all_to_all.26 = f32[64,2,1536]{2,1,0:T(2,128)S(1)} all-to-all(f32[64,2,1536]{2,1,0:T(2,128)S(1)} %copy.88), channel_id=1, replica_groups=mesh['req'=64,'kv'=2] {'req'}, dimensions={0} | all-to-all | bytes 1572864 | tf_op jit(solution)/shard_map/all_to_all | solution.py:148
  217.8 1.2 fusion.1
  (83 shorter events, 14.5 us)
Async XLA Ops:
  6.5 138.2 %copy-start = (bf16[768,1536]{1,0:T(8,128)(2,1)S(1)}, bf16[768,1536]{1,0:T(8,128)(2,1)}, u32[]{:S(2)}) copy-start(bf16[768,1536]{1,0:T(8,128)(2,1)} %param.28) | copy-start | bytes 7077892
  83.9 6.7 %copy-start.12 = (s32[64]{0:T(128)S(1)}, s32[64]{0:T(128)}, u32[]{:S(2)}) copy-start(s32[64]{0:T(128)} %param.33) | copy-start | bytes 772
  83.9 9.2 %copy-start.9 = (bf16[1536]{0:T(1024)(128)(2,1)S(1)}, bf16[1536]{0:T(1024)(128)(2,1)}, u32[]{:S(2)}) copy-start(bf16[1536]{0:T(1024)(128)(2,1)} %param.24) | copy-start | bytes 9220
  83.9 9.3 %copy-start.2 = (bf16[16,1536]{1,0:T(8,128)(2,1)S(1)}, bf16[16,1536]{1,0:T(8,128)(2,1)}, u32[]{:S(2)}) copy-start(bf16[16,1536]{1,0:T(8,128)(2,1)} %param.23) | copy-start | bytes 147460
  83.9 57.3 %all-to-all-start.1 = ((bf16[64,256,128]{2,1,0:T(8,128)(2,1)}), bf16[64,256,128]{2,1,0:T(8,128)(2,1)}, u32[]{:S(2)}, u32[]{:S(2)}) async-start(bf16[64,256,128]{2,1,0:T(8,128)(2,1)} %get-tuple-element.49), calls=%async_computation.1 | async-start | bytes 8388608 | tf_op jit(solution)/shard_map/all_to_all | solution.py:99
  90.5 7.3 %copy-start.4 = (bf16[1536,128]{1,0:T(8,128)(2,1)S(1)}, bf16[1536,128]{1,0:T(8,128)(2,1)}, u32[]{:S(2)}) copy-start(bf16[1536,128]{1,0:T(8,128)(2,1)} %param.26) | copy-start | bytes 1179652
  90.5 7.6 %copy-start.5 = (bf16[1536,128]{1,0:T(8,128)(2,1)S(1)}, bf16[1536,128]{1,0:T(8,128)(2,1)}, u32[]{:S(2)}) copy-start(bf16[1536,128]{1,0:T(8,128)(2,1)} %param.27) | copy-start | bytes 1179652
  90.5 64.1 %reduce-scatter.2.cloned.1.call-start = ((), (), s32[]{:S(2)}) async-start(), calls=%async_computation.6 | async-start | bytes 147456 | tf_op jit(solution)/shard_map/reduce_scatter | solution.py:107
  144.7 2.6 %copy-start.8 = (s32[8,4]{0,1:T(4,128)S(1)}, s32[8,4]{0,1:T(4,128)}, u32[]{:S(2)}) copy-start(s32[8,4]{0,1:T(4,128)} %param.36) | copy-start | bytes 388
  144.7 2.8 %copy-start.10 = (bf16[1536]{0:T(1024)(128)(2,1)S(1)}, bf16[1536]{0:T(1024)(128)(2,1)}, u32[]{:S(2)}) copy-start(bf16[1536]{0:T(1024)(128)(2,1)} %param.34) | copy-start | bytes 9220
  144.7 10.8 %copy-start.11 = (bf16[1536,32]{0,1:T(8,128)(2,1)S(1)}, bf16[1536,32]{0,1:T(8,128)(2,1)}, u32[]{:S(2)}) copy-start(bf16[1536,32]{0,1:T(8,128)(2,1)} %param.35) | copy-start | bytes 294916
  145.8 41.9 %all-gather.5.cloned.1.call-start = ((), (), s32[]{:S(2)}) async-start(), calls=%async_computation.8 | async-start | bytes 1769472 | tf_op jit(solution)/shard_map/all_gather | solution.py:134
  146.6 43.7 %all-gather.3.cloned.1.call-start = ((), (), s32[]{:S(2)}) async-start(), calls=%async_computation.7 | async-start | bytes 1769472 | tf_op jit(solution)/shard_map/all_gather | solution.py:133
  155.5 1.6 copy-start.6
  155.7 13.4 %copy-start.3 = (bf16[1,1536,192]{1,2,0:T(8,128)(2,1)S(1)}, bf16[1,1536,192]{1,2,0:T(8,128)(2,1)}, u32[]{:S(2)}) copy-start(bf16[1,1536,192]{1,2,0:T(8,128)(2,1)} %param.39) | copy-start | bytes 1769476
  158.5 22.9 %all-to-all-start.2 = ((bf16[64,2,1536]{2,1,0:T(2,128)(2,1)}), bf16[64,2,1536]{2,1,0:T(2,128)(2,1)S(1)}, u32[]{:S(2)}, u32[]{:S(2)}) async-start(bf16[64,2,1536]{2,1,0:T(2,128)(2,1)} %copy.84), calls=%async_computation.3 | async-start | bytes 786432 | tf_op jit(solution)/shard_map/all_to_all | solution.py:139
  181.5 0.7 copy-start.1
  182.2 12.2 %all-to-all-start.3 = ((bf16[2,1,1536,192]{2,3,1,0:T(8,128)(2,1)}), bf16[2,1,1536,192]{2,3,1,0:T(8,128)(2,1)S(1)}, u32[]{:S(2)}, u32[]{:S(2)}) async-start(bf16[2,1,1536,192]{2,3,1,0:T(8,128)(2,1)} %pad_maximum_fusion), calls=%async_computation.4 | async-start | bytes 2359296 | tf_op jit(solution)/shard_map/all_to_all | solution.py:136
  194.4 23.4 %copy-start.7 = (bf16[8,1536]{1,0:T(8,128)(2,1)S(1)}, bf16[8,1536]{1,0:T(8,128)(2,1)}, u32[]{:S(2)}) copy-start(bf16[8,1536]{1,0:T(8,128)(2,1)} %copy-done.6) | copy-start | bytes 73732
Sparse Core Ops, SparseCore 0:
  145.9 8.5 reduce-scatter.1
  156.2 13.4 all-gather.4
  171.3 13.2 all-gather.2
